TPU v7x, 256 devices: a whole 4x4x8 slice. The times are simulated.
256 devices in a mesh: group: 8 (over x, core), prompt: 32 (over z, y).
Axes of the slice: x: 4, y: 4, z: 8, core: 2. Of those that a mesh axis runs over, the one named last changes fastest.
Arguments:
- queries: bfloat16 [32, 8, 64, 3072], P('prompt', 'group'), may hold values from -48 to 48
- fresh_latent: bfloat16 [32, 8, 64, 576], P('prompt', 'group'), may hold values from -6 to 6
- latent_cache: bfloat16 [32, 8, 512, 576], P('prompt', 'group'), may hold values from -48 to 48
- selected: int32 [32, 8, 64], P('prompt', 'group'), may hold values from 0 to 511, as said below
- position: int32 [32, 8], P('prompt'), may hold values from 0 to 7, each once within a row
- latent_gain: bfloat16 [512], replicated, may hold values from 0.099609375 to 1.8984375
- kv_up: bfloat16 [512, 4096], P('prompt'), may hold values from -0.25 to 0.25
- out_weight: bfloat16 [2048, 2048], P('prompt'), may hold values from -0.125 to 0.125
Outputs:
- attended: bfloat16 [32, 8, 64, 2048], P('prompt', 'group')
- blended: bfloat16 [32, 8, 512, 576], P('prompt', 'group')
Inputs may be any that keep to these rules, and one draw needn't show every extreme that they name: `selected`: the 64 indices of a group are distinct and increasing.
All inputs are finite; a program needn't handle non-finite values.
Results may differ from a plain program's by a relative error of at most 0.011.
Values may be sent and summed in bfloat16 or wider, within the bound.
A program may use at most 128 MiB of HBM per device.

v0:
```python
import jax
import jax.numpy as jnp
from jax import lax
from jax.sharding import Mesh
from jax.sharding import PartitionSpec as P

D = 2048
H = 16
DN = 128
DR = 64
DV = 128
LAT = 512
PROMPT = ("prompt_0", "prompt_1")


def whole_of(array, axes, dim):
    whole = array
    for number in range(len(axes) - 1, -1, -1):
        whole = lax.all_gather(whole, axes[number], axis=dim, tiled=True)
    return whole


def rope_rotate(values, places):
    half = values.shape[-1] // 2
    freqs = 10000.0 ** (-jnp.arange(half, dtype=jnp.float32) / half)
    angles = places[..., None] * freqs
    cosine = jnp.cos(angles)
    sine = jnp.sin(angles)
    first = values[..., :half]
    second = values[..., half:]
    return jnp.concatenate([first * cosine - second * sine, second * cosine + first * sine], -1)


def prepare_rows(fresh, gain, places):
    latent = fresh[..., :LAT].astype(jnp.float32)
    factor = lax.rsqrt(jnp.mean(latent * latent, -1, keepdims=True) + 1e-06)
    normed = latent * factor * gain.astype(jnp.float32)
    turned = rope_rotate(fresh[..., LAT:].astype(jnp.float32), places)
    return jnp.concatenate([normed, turned], -1).astype(jnp.bfloat16)


def shards(queries, fresh_latent, latent_cache, selected, position, latent_gain, kv_up, out_weight):
    prompts, groups, picks, _ = queries.shape
    length = latent_cache.shape[2]
    first_group = lax.axis_index("group") * groups
    own_order = lax.dynamic_slice_in_dim(position, first_group, groups, 1)
    place_int = own_order[:, :, None] * length + selected
    places = place_int.astype(jnp.float32)
    fresh_rows = prepare_rows(fresh_latent, latent_gain, places)
    prompt_ids = jnp.arange(prompts, dtype=jnp.int32)[:, None, None]
    group_ids = jnp.arange(groups, dtype=jnp.int32)[None, :, None]
    blended = latent_cache.at[prompt_ids, group_ids, selected].set(fresh_rows)
    whole_kv = whole_of(kv_up, PROMPT, 0).reshape(LAT, H, DN + DV)
    shaped = queries.reshape(prompts, groups, picks, H, DN + DR)
    absorbed = jnp.einsum(
        "pcshd,lhd->pcshl", shaped[..., :DN], whole_kv[..., :DN], preferred_element_type=jnp.float32
    ).astype(jnp.bfloat16)
    turned = rope_rotate(shaped[..., DN:].astype(jnp.float32), places[..., None]).astype(
        jnp.bfloat16
    )
    rows = groups * picks
    query_vec = jnp.concatenate([absorbed, turned], -1).reshape(prompts, rows, H, LAT + DR)
    query_place = place_int.reshape(prompts, rows)
    scale = (DN + DR) ** (-0.5)
    offsets = jnp.arange(length, dtype=jnp.int32)

    def update(state, keys, key_place):
        peak, total, mixed = state
        allowed = (key_place[:, None, :] <= query_place[:, :, None])[:, :, None, :]
        scores = (
            jnp.einsum("pqhe,pke->pqhk", query_vec, keys, preferred_element_type=jnp.float32)
            * scale
        )
        block_peak = jnp.max(jnp.where(allowed, scores, -1e30), -1)
        new_peak = jnp.maximum(peak, block_peak)
        probs = jnp.where(allowed, jnp.exp(scores - new_peak[..., None]), 0.0)
        decay = jnp.exp(peak - new_peak)
        total = total * decay + jnp.sum(probs, -1)
        mixed = mixed * decay[..., None] + jnp.einsum(
            "pqhk,pkl->pqhl",
            probs.astype(jnp.bfloat16),
            keys[..., :LAT],
            preferred_element_type=jnp.float32,
        )
        return (new_peak, total, mixed)

    start_state = (
        jnp.full((prompts, rows, H), -1e30, jnp.float32),
        jnp.zeros((prompts, rows, H), jnp.float32),
        jnp.zeros((prompts, rows, H, LAT), jnp.float32),
    )
    piece = lax.all_gather(blended, "group", axis=1, tiled=True)

    def one_group(index, carry):
        keys = lax.dynamic_slice_in_dim(piece, index, 1, 1)[:, 0]
        order = lax.dynamic_slice_in_dim(position, index, 1, 1)
        key_place = order * length + offsets[None, :]
        needed = jnp.any(key_place[:, :1] <= jnp.max(query_place, -1, keepdims=True))
        return lax.cond(needed, lambda c: update(c, keys, key_place), lambda c: c, carry)

    peak, total, mixed = lax.fori_loop(0, piece.shape[1], one_group, start_state)
    latent_mix = (mixed / total[..., None]).astype(jnp.bfloat16)
    heads = jnp.einsum(
        "pqhl,lhv->pqhv", latent_mix, whole_kv[..., DN:], preferred_element_type=jnp.float32
    ).astype(jnp.bfloat16)
    heads = heads.reshape(prompts * rows, H * DV)
    whole_out = lax.all_gather(out_weight, PROMPT, axis=0, tiled=True)
    attended = jnp.dot(heads, whole_out, preferred_element_type=jnp.float32)
    return (attended.astype(jnp.bfloat16).reshape(prompts, groups, picks, D), blended)


def solution(mesh):
    split = Mesh(mesh.devices.reshape(mesh.shape["group"], 8, 4), ("group", "prompt_0", "prompt_1"))
    return jax.shard_map(
        shards,
        mesh=split,
        in_specs=(
            P(PROMPT, "group", None, None),
            P(PROMPT, "group", None, None),
            P(PROMPT, "group", None, None),
            P(PROMPT, "group", None),
            P(PROMPT, None),
            P(),
            P(PROMPT, None),
            P(PROMPT, None),
        ),
        out_specs=(P(PROMPT, "group", None, None), P(PROMPT, "group", None, None)),
        check_vma=False,
    )
```

profile of v0, /device:TPU:57, one launch (start us, length us, event | category | flops | bytes accessed | tf_op | source)
XLA Modules:
  0.0 239.9 jit_solution(15318648085517091847)
XLA Ops:
  7.2 10.8 %all_gather.13 = bf16[64,4096]{1,0:T(8,128)(2,1)} all-gather(bf16[16,4096]{1,0:T(8,128)(2,1)} %param.18), channel_id=1, replica_groups=mesh['group'=8,'prompt_0'=8,'prompt_1'=4] {'prompt_1'}, dimensions={0}, use_global_device_ids=true | all-gather | bytes 655360 | tf_op jit(solution)/shard_map/all_gather | solution.py:19
  19.0 1.2 fusion.52
  20.3 1.3 convert_bitcast_fusion
  21.9 1.4 copy.49
  23.6 1.3 scatter_custom_fusion
  29.4 46.8 %all-gather.5.cloned.1.call-done = bf16[512,4096]{1,0:T(8,128)(2,1)} async-done(((bf16[64,4096]{1,0:T(8,128)(2,1)}), bf16[512,4096]{1,0:T(8,128)(2,1)}) %all-gather.5.cloned.1.call-update) | async-done | bytes 4194320 | tf_op jit(solution)/shard_map/all_gather | solution.py:19
  76.2 6.5 %copy.53 = bf16[512,4096]{0,1:T(8,128)(2,1)} copy(bf16[512,4096]{1,0:T(8,128)(2,1)} %all-gather.5.cloned.1.call-done) | data formatting | bytes 8388608 | tf_op jit(solution)/shard_map/all_gather | solution.py:19
  82.7 2.0 fusion.20
  84.8 1.3 maximum_bitcast_fusion
  86.1 31.9 %all-gather.9.cloned.1.call-done = bf16[4096,576]{1,0:T(8,128)(2,1)} async-done(((bf16[512,576]{1,0:T(8,128)(2,1)}), bf16[4096,576]{1,0:T(8,128)(2,1)}) %all-gather.9.cloned.1.call-update) | async-done | bytes 4718608 | tf_op jit(solution)/shard_map/all_gather | solution.py:92
  118.0 7.7 %copy.57 = bf16[1,8,512,576]{2,3,1,0:T(8,128)(2,1)} copy(bf16[1,8,512,576]{3,2,1,0:T(8,128)(2,1)} %bitcast.103) | data formatting | bytes 9437184
  126.3 98.4 %while.20 = (s32[]{:T(128)}, f32[1,64,16]{1,2,0:T(8,128)S(1)}, f32[1,64,16]{1,2,0:T(8,128)S(1)}, f32[1,64,16,512]{3,2,1,0:T(8,128)S(1)}, s32[1,8]{1,0:T(1,128)S(...) while((s32[]{:T(128)}, f32[1,64,16]{1,2,0:T(8,128)S(1)}, ...), condition=%wide.region_8.9_spmd.clone, body=%wide.region_3.8_spmd.clone.sunk | while | flops 1146129920 | bytes 17670692 | solution.py:101
  129.5 9.0 %conditional.3 = ((f32[1,64,16]{1,2,0:T(8,128)S(1)}, f32[1,64,16]{1,2,0:T(8,128)S(1)}, f32[1,64,16,512]{3,2,1,0:T(8,128)S(1)})) conditional(s32[]{:T(128)} %bitcast.97, (f32[1,64,16]{1,2,0:T(8,128)S(1)}, f32[1,64,16]{1,2,0:T(8,128)S(1)}, f32[1,64,16,512]{3,2,1,0:T(8,128)S(1)}) %tuple.70, (s32[1,512]{1,0:T(1,128)S(1)}, s32[1,1,64]{2,1,0:T(1,128)S(1)}, ...), branch_computations={%region_4.0_spmd, %region_5.7_spmd} | conditional | flops 1146129408 | bytes 17668416 | solution.py:99
  130.8 2.5 %fusion.2 = (f32[64,16]{0,1:T(8,128)S(1)}, f32[512,64,16]{0,1,2:T(8,128)S(1)}) fusion(pred[64,512]{1,0:T(8,128)(4,1)S(1)} %broadcast_compare_fusion, bf16[1,64,16,576]{3,1,2,0:T(8,128)(2,1)} %get-tuple-element.279, bf16[1,1,512,576]{2,3,1,0:T(8,128)(2,1)S(1)} %constant_dynamic-slice_fusion), kind=kOutput, calls=%fused_computation.5 | convolution fusion | flops 605551616 | bytes 3903488 | tf_op jit(solution)/shard_map/while/body/eval_jaxpr/cond/branch_1_fun/pqhe,pke->pqhk/dot_general | solution.py:71
  134.1 2.2 copy.47
  136.3 2.2 bitcast_add_fusion
  141.8 9.1 %conditional.3 = ((f32[1,64,16]{1,2,0:T(8,128)S(1)}, f32[1,64,16]{1,2,0:T(8,128)S(1)}, f32[1,64,16,512]{3,2,1,0:T(8,128)S(1)})) conditional(s32[]{:T(128)} %bitcast.97, (f32[1,64,16]{1,2,0:T(8,128)S(1)}, f32[1,64,16]{1,2,0:T(8,128)S(1)}, f32[1,64,16,512]{3,2,1,0:T(8,128)S(1)}) %tuple.70, (s32[1,512]{1,0:T(1,128)S(1)}, s32[1,1,64]{2,1,0:T(1,128)S(1)}, ...), branch_computations={%region_4.0_spmd, %region_5.7_spmd} | conditional | flops 1146129408 | bytes 17668416 | solution.py:99
  143.1 2.5 %fusion.2 = (f32[64,16]{0,1:T(8,128)S(1)}, f32[512,64,16]{0,1,2:T(8,128)S(1)}) fusion(pred[64,512]{1,0:T(8,128)(4,1)S(1)} %broadcast_compare_fusion, bf16[1,64,16,576]{3,1,2,0:T(8,128)(2,1)} %get-tuple-element.279, bf16[1,1,512,576]{2,3,1,0:T(8,128)(2,1)S(1)} %constant_dynamic-slice_fusion), kind=kOutput, calls=%fused_computation.5 | convolution fusion | flops 605551616 | bytes 3903488 | tf_op jit(solution)/shard_map/while/body/eval_jaxpr/cond/branch_1_fun/pqhe,pke->pqhk/dot_general | solution.py:71
  146.4 2.2 copy.47
  148.7 2.2 bitcast_add_fusion
  154.1 9.0 %conditional.3 = ((f32[1,64,16]{1,2,0:T(8,128)S(1)}, f32[1,64,16]{1,2,0:T(8,128)S(1)}, f32[1,64,16,512]{3,2,1,0:T(8,128)S(1)})) conditional(s32[]{:T(128)} %bitcast.97, (f32[1,64,16]{1,2,0:T(8,128)S(1)}, f32[1,64,16]{1,2,0:T(8,128)S(1)}, f32[1,64,16,512]{3,2,1,0:T(8,128)S(1)}) %tuple.70, (s32[1,512]{1,0:T(1,128)S(1)}, s32[1,1,64]{2,1,0:T(1,128)S(1)}, ...), branch_computations={%region_4.0_spmd, %region_5.7_spmd} | conditional | flops 1146129408 | bytes 17668416 | solution.py:99
  155.4 2.5 %fusion.2 = (f32[64,16]{0,1:T(8,128)S(1)}, f32[512,64,16]{0,1,2:T(8,128)S(1)}) fusion(pred[64,512]{1,0:T(8,128)(4,1)S(1)} %broadcast_compare_fusion, bf16[1,64,16,576]{3,1,2,0:T(8,128)(2,1)} %get-tuple-element.279, bf16[1,1,512,576]{2,3,1,0:T(8,128)(2,1)S(1)} %constant_dynamic-slice_fusion), kind=kOutput, calls=%fused_computation.5 | convolution fusion | flops 605551616 | bytes 3903488 | tf_op jit(solution)/shard_map/while/body/eval_jaxpr/cond/branch_1_fun/pqhe,pke->pqhk/dot_general | solution.py:71
  158.7 2.2 copy.47
  160.9 2.2 bitcast_add_fusion
  166.4 9.2 %conditional.3 = ((f32[1,64,16]{1,2,0:T(8,128)S(1)}, f32[1,64,16]{1,2,0:T(8,128)S(1)}, f32[1,64,16,512]{3,2,1,0:T(8,128)S(1)})) conditional(s32[]{:T(128)} %bitcast.97, (f32[1,64,16]{1,2,0:T(8,128)S(1)}, f32[1,64,16]{1,2,0:T(8,128)S(1)}, f32[1,64,16,512]{3,2,1,0:T(8,128)S(1)}) %tuple.70, (s32[1,512]{1,0:T(1,128)S(1)}, s32[1,1,64]{2,1,0:T(1,128)S(1)}, ...), branch_computations={%region_4.0_spmd, %region_5.7_spmd} | conditional | flops 1146129408 | bytes 17668416 | solution.py:99
  167.6 2.5 %fusion.2 = (f32[64,16]{0,1:T(8,128)S(1)}, f32[512,64,16]{0,1,2:T(8,128)S(1)}) fusion(pred[64,512]{1,0:T(8,128)(4,1)S(1)} %broadcast_compare_fusion, bf16[1,64,16,576]{3,1,2,0:T(8,128)(2,1)} %get-tuple-element.279, bf16[1,1,512,576]{2,3,1,0:T(8,128)(2,1)S(1)} %constant_dynamic-slice_fusion), kind=kOutput, calls=%fused_computation.5 | convolution fusion | flops 605551616 | bytes 3903488 | tf_op jit(solution)/shard_map/while/body/eval_jaxpr/cond/branch_1_fun/pqhe,pke->pqhk/dot_general | solution.py:71
  171.0 2.3 copy.47
  173.3 2.2 bitcast_add_fusion
  178.8 9.1 %conditional.3 = ((f32[1,64,16]{1,2,0:T(8,128)S(1)}, f32[1,64,16]{1,2,0:T(8,128)S(1)}, f32[1,64,16,512]{3,2,1,0:T(8,128)S(1)})) conditional(s32[]{:T(128)} %bitcast.97, (f32[1,64,16]{1,2,0:T(8,128)S(1)}, f32[1,64,16]{1,2,0:T(8,128)S(1)}, f32[1,64,16,512]{3,2,1,0:T(8,128)S(1)}) %tuple.70, (s32[1,512]{1,0:T(1,128)S(1)}, s32[1,1,64]{2,1,0:T(1,128)S(1)}, ...), branch_computations={%region_4.0_spmd, %region_5.7_spmd} | conditional | flops 1146129408 | bytes 17668416 | solution.py:99
  178.8 1.1 constant_dynamic-slice_fusion
  180.0 2.5 %fusion.2 = (f32[64,16]{0,1:T(8,128)S(1)}, f32[512,64,16]{0,1,2:T(8,128)S(1)}) fusion(pred[64,512]{1,0:T(8,128)(4,1)S(1)} %broadcast_compare_fusion, bf16[1,64,16,576]{3,1,2,0:T(8,128)(2,1)} %get-tuple-element.279, bf16[1,1,512,576]{2,3,1,0:T(8,128)(2,1)S(1)} %constant_dynamic-slice_fusion), kind=kOutput, calls=%fused_computation.5 | convolution fusion | flops 605551616 | bytes 3903488 | tf_op jit(solution)/shard_map/while/body/eval_jaxpr/cond/branch_1_fun/pqhe,pke->pqhk/dot_general | solution.py:71
  183.4 2.2 copy.47
  185.6 2.2 bitcast_add_fusion
  191.1 9.1 %conditional.3 = ((f32[1,64,16]{1,2,0:T(8,128)S(1)}, f32[1,64,16]{1,2,0:T(8,128)S(1)}, f32[1,64,16,512]{3,2,1,0:T(8,128)S(1)})) conditional(s32[]{:T(128)} %bitcast.97, (f32[1,64,16]{1,2,0:T(8,128)S(1)}, f32[1,64,16]{1,2,0:T(8,128)S(1)}, f32[1,64,16,512]{3,2,1,0:T(8,128)S(1)}) %tuple.70, (s32[1,512]{1,0:T(1,128)S(1)}, s32[1,1,64]{2,1,0:T(1,128)S(1)}, ...), branch_computations={%region_4.0_spmd, %region_5.7_spmd} | conditional | flops 1146129408 | bytes 17668416 | solution.py:99
  192.3 2.6 %fusion.2 = (f32[64,16]{0,1:T(8,128)S(1)}, f32[512,64,16]{0,1,2:T(8,128)S(1)}) fusion(pred[64,512]{1,0:T(8,128)(4,1)S(1)} %broadcast_compare_fusion, bf16[1,64,16,576]{3,1,2,0:T(8,128)(2,1)} %get-tuple-element.279, bf16[1,1,512,576]{2,3,1,0:T(8,128)(2,1)S(1)} %constant_dynamic-slice_fusion), kind=kOutput, calls=%fused_computation.5 | convolution fusion | flops 605551616 | bytes 3903488 | tf_op jit(solution)/shard_map/while/body/eval_jaxpr/cond/branch_1_fun/pqhe,pke->pqhk/dot_general | solution.py:71
  195.7 2.2 copy.47
  197.9 2.2 bitcast_add_fusion
  203.4 9.1 %conditional.3 = ((f32[1,64,16]{1,2,0:T(8,128)S(1)}, f32[1,64,16]{1,2,0:T(8,128)S(1)}, f32[1,64,16,512]{3,2,1,0:T(8,128)S(1)})) conditional(s32[]{:T(128)} %bitcast.97, (f32[1,64,16]{1,2,0:T(8,128)S(1)}, f32[1,64,16]{1,2,0:T(8,128)S(1)}, f32[1,64,16,512]{3,2,1,0:T(8,128)S(1)}) %tuple.70, (s32[1,512]{1,0:T(1,128)S(1)}, s32[1,1,64]{2,1,0:T(1,128)S(1)}, ...), branch_computations={%region_4.0_spmd, %region_5.7_spmd} | conditional | flops 1146129408 | bytes 17668416 | solution.py:99
  203.4 1.1 constant_dynamic-slice_fusion
  204.7 2.5 %fusion.2 = (f32[64,16]{0,1:T(8,128)S(1)}, f32[512,64,16]{0,1,2:T(8,128)S(1)}) fusion(pred[64,512]{1,0:T(8,128)(4,1)S(1)} %broadcast_compare_fusion, bf16[1,64,16,576]{3,1,2,0:T(8,128)(2,1)} %get-tuple-element.279, bf16[1,1,512,576]{2,3,1,0:T(8,128)(2,1)S(1)} %constant_dynamic-slice_fusion), kind=kOutput, calls=%fused_computation.5 | convolution fusion | flops 605551616 | bytes 3903488 | tf_op jit(solution)/shard_map/while/body/eval_jaxpr/cond/branch_1_fun/pqhe,pke->pqhk/dot_general | solution.py:71
  208.0 2.2 copy.47
  210.2 2.2 bitcast_add_fusion
  215.7 9.0 %conditional.3 = ((f32[1,64,16]{1,2,0:T(8,128)S(1)}, f32[1,64,16]{1,2,0:T(8,128)S(1)}, f32[1,64,16,512]{3,2,1,0:T(8,128)S(1)})) conditional(s32[]{:T(128)} %bitcast.97, (f32[1,64,16]{1,2,0:T(8,128)S(1)}, f32[1,64,16]{1,2,0:T(8,128)S(1)}, f32[1,64,16,512]{3,2,1,0:T(8,128)S(1)}) %tuple.70, (s32[1,512]{1,0:T(1,128)S(1)}, s32[1,1,64]{2,1,0:T(1,128)S(1)}, ...), branch_computations={%region_4.0_spmd, %region_5.7_spmd} | conditional | flops 1146129408 | bytes 17668416 | solution.py:99
  216.9 2.5 %fusion.2 = (f32[64,16]{0,1:T(8,128)S(1)}, f32[512,64,16]{0,1,2:T(8,128)S(1)}) fusion(pred[64,512]{1,0:T(8,128)(4,1)S(1)} %broadcast_compare_fusion, bf16[1,64,16,576]{3,1,2,0:T(8,128)(2,1)} %get-tuple-element.279, bf16[1,1,512,576]{2,3,1,0:T(8,128)(2,1)S(1)} %constant_dynamic-slice_fusion), kind=kOutput, calls=%fused_computation.5 | convolution fusion | flops 605551616 | bytes 3903488 | tf_op jit(solution)/shard_map/while/body/eval_jaxpr/cond/branch_1_fun/pqhe,pke->pqhk/dot_general | solution.py:71
  220.3 2.2 copy.47
  222.5 2.2 bitcast_add_fusion
  225.1 2.4 %fusion.26 = bf16[1,64,16,128]{3,1,2,0:T(8,128)(2,1)S(1)} fusion(bf16[512,16,256]{0,2,1:T(8,128)(2,1)} %bitcast.100, bf16[64,16,512]{2,1,0:T(8,128)(2,1)S(1)} %fusion.30), kind=kOutput, calls=%fused_computation.34 | convolution fusion | flops 134348800 | bytes 3407872 | tf_op jit(solution)/shard_map/pqhl,lhv->pqhv/dot_general | solution.py:103
  227.7 5.7 %fusion.12 = bf16[1,1,64,2048]{3,2,1,0:T(8,128)(2,1)} fusion(bf16[2048,2048]{1,0:T(8,128)(2,1)} %all-gather.7.cloned.1.call-done, bf16[8,8,16,128]{3,2,1,0:T(8,128)(2,1)S(1)} %bitcast.105), kind=kOutput, calls=%fused_computation.24 | convolution fusion | flops 537001984 | bytes 8912896 | tf_op jit(solution)/shard_map/dot_general | solution.py:108
  (143 shorter events, 36.5 us)
Async XLA Ops:
  7.2 16.2 %copy-start.5 = (bf16[1,1,64,576]{3,2,1,0:T(8,128)(2,1)S(1)}, bf16[1,1,64,576]{3,2,1,0:T(8,128)(2,1)}, u32[]{:S(2)}) copy-start(bf16[1,1,64,576]{3,2,1,0:T(8,128)(2,1)} %param.13) | copy-start | bytes 221188
  7.2 16.1 %copy-start.6 = (bf16[512]{0:T(512)(128)(2,1)S(1)}, bf16[512]{0:T(512)(128)(2,1)}, u32[]{:S(2)}) copy-start(bf16[512]{0:T(512)(128)(2,1)} %param.17) | copy-start | bytes 3076
  7.2 69.0 %all-gather.5.cloned.1.call-start = ((), (), s32[]{:S(2)}) async-start(), calls=%async_computation | async-start | bytes 4718592 | tf_op jit(solution)/shard_map/all_gather | solution.py:19
  18.1 8.4 %copy-start.4 = (bf16[1,1,64,3072]{3,2,1,0:T(8,128)(2,1)S(1)}, bf16[1,1,64,3072]{3,2,1,0:T(8,128)(2,1)}, u32[]{:S(2)}) copy-start(bf16[1,1,64,3072]{3,2,1,0:T(8,128)(2,1)} %param.12) | copy-start | bytes 1179652
  18.1 99.9 %all-gather.9.cloned.1.call-start = ((), (), s32[]{:S(2)}) async-start(), calls=%async_computation.2 | async-start | bytes 5898240 | tf_op jit(solution)/shard_map/all_gather | solution.py:92
  24.9 0.8 copy-start.1
  25.8 1.4 copy-start.2
  25.8 201.9 %all-gather.7.cloned.1.call-start = ((), (), s32[]{:S(2)}) async-start(), calls=%async_computation.1 | async-start | bytes 8650752 | tf_op jit(solution)/shard_map/all_gather | solution.py:107
  27.1 2.3 copy-start.3
  76.2 6.5 %slice-start = ((bf16[1,1,64,16,192]{4,3,2,1,0:T(8,128)(2,1)}), bf16[1,1,64,16,128]{4,3,2,1,0:T(8,128)(2,1)S(1)}, s32[]{:S(2)}) async-start(bf16[1,1,64,16,192]{4,3,2,1,0:T(8,128)(2,1)} %copy-done.3), calls=%async_computation.3 | async-start | bytes 524288 | tf_op jit(solution)/shard_map/slice | solution.py:56
  125.7 0.7 copy-start.7
  130.7 2.6 %copy-start = (bf16[1,1,512,576]{2,3,1,0:T(8,128)(2,1)}, bf16[1,1,512,576]{2,3,1,0:T(8,128)(2,1)S(1)}, u32[]{:S(2)}) copy-start(bf16[1,1,512,576]{2,3,1,0:T(8,128)(2,1)S(1)} %constant_dynamic-slice_fusion) | copy-start | bytes 1769476 | tf_op jit(solution)/shard_map/while/body/eval_jaxpr/cond
  143.0 2.7 %copy-start = (bf16[1,1,512,576]{2,3,1,0:T(8,128)(2,1)}, bf16[1,1,512,576]{2,3,1,0:T(8,128)(2,1)S(1)}, u32[]{:S(2)}) copy-start(bf16[1,1,512,576]{2,3,1,0:T(8,128)(2,1)S(1)} %constant_dynamic-slice_fusion) | copy-start | bytes 1769476 | tf_op jit(solution)/shard_map/while/body/eval_jaxpr/cond
  155.3 2.6 %copy-start = (bf16[1,1,512,576]{2,3,1,0:T(8,128)(2,1)}, bf16[1,1,512,576]{2,3,1,0:T(8,128)(2,1)S(1)}, u32[]{:S(2)}) copy-start(bf16[1,1,512,576]{2,3,1,0:T(8,128)(2,1)S(1)} %constant_dynamic-slice_fusion) | copy-start | bytes 1769476 | tf_op jit(solution)/shard_map/while/body/eval_jaxpr/cond
  167.5 2.6 %copy-start = (bf16[1,1,512,576]{2,3,1,0:T(8,128)(2,1)}, bf16[1,1,512,576]{2,3,1,0:T(8,128)(2,1)S(1)}, u32[]{:S(2)}) copy-start(bf16[1,1,512,576]{2,3,1,0:T(8,128)(2,1)S(1)} %constant_dynamic-slice_fusion) | copy-start | bytes 1769476 | tf_op jit(solution)/shard_map/while/body/eval_jaxpr/cond
  179.9 2.6 %copy-start = (bf16[1,1,512,576]{2,3,1,0:T(8,128)(2,1)}, bf16[1,1,512,576]{2,3,1,0:T(8,128)(2,1)S(1)}, u32[]{:S(2)}) copy-start(bf16[1,1,512,576]{2,3,1,0:T(8,128)(2,1)S(1)} %constant_dynamic-slice_fusion) | copy-start | bytes 1769476 | tf_op jit(solution)/shard_map/while/body/eval_jaxpr/cond
  192.2 2.7 %copy-start = (bf16[1,1,512,576]{2,3,1,0:T(8,128)(2,1)}, bf16[1,1,512,576]{2,3,1,0:T(8,128)(2,1)S(1)}, u32[]{:S(2)}) copy-start(bf16[1,1,512,576]{2,3,1,0:T(8,128)(2,1)S(1)} %constant_dynamic-slice_fusion) | copy-start | bytes 1769476 | tf_op jit(solution)/shard_map/while/body/eval_jaxpr/cond
  204.6 2.6 %copy-start = (bf16[1,1,512,576]{2,3,1,0:T(8,128)(2,1)}, bf16[1,1,512,576]{2,3,1,0:T(8,128)(2,1)S(1)}, u32[]{:S(2)}) copy-start(bf16[1,1,512,576]{2,3,1,0:T(8,128)(2,1)S(1)} %constant_dynamic-slice_fusion) | copy-start | bytes 1769476 | tf_op jit(solution)/shard_map/while/body/eval_jaxpr/cond
  216.8 2.6 %copy-start = (bf16[1,1,512,576]{2,3,1,0:T(8,128)(2,1)}, bf16[1,1,512,576]{2,3,1,0:T(8,128)(2,1)S(1)}, u32[]{:S(2)}) copy-start(bf16[1,1,512,576]{2,3,1,0:T(8,128)(2,1)S(1)} %constant_dynamic-slice_fusion) | copy-start | bytes 1769476 | tf_op jit(solution)/shard_map/while/body/eval_jaxpr/cond
Sparse Core Ops, SparseCore 0:
  18.2 57.9 all-gather.4
  78.0 39.9 all-gather.8
  120.6 93.4 all-gather.6
where the time goes:
time: 242 us; the launch traced here: 240 us
  waiting for transfers between devices  79.4 us (33%)
  local copies, waits for them, and re-layouts  52.4 us (22%)
  matrix products  48.2 us (20%)
  other arithmetic  24.2 us (10%)
  between operations  14 us (6%)
  blocking collectives  10.8 us (4%)
  loops' own time  10.8 us (4%)
    all_gather x1, waiting for transfers between devices, whole_of(): whole = lax.all_gather(whole, axes[number], axis=dim, tiled=True)  46.8 us
    all_gather x1, waiting for transfers between devices, shards(): piece = lax.all_gather(blended, 'group', axis=1, tiled=True)  31.9 us
    dynamic_slice x16, local copies, waits for them, and re-layouts, one_group(): keys = lax.dynamic_slice_in_dim(piece, index, 1, 1)[:, 0]  26.8 us
    dot_general x8, matrix products, update(): jnp.einsum('pqhe,pke->pqhk', query_vec, keys, preferred_element_type=jnp....  20.2 us
    dot_general x8, matrix products, update(): jnp.einsum('pqhk,pkl->pqhl', probs.astype(jnp.bfloat16), keys[..., :LAT],...  17.9 us
    unnamed x18, local copies, waits for them, and re-layouts  11.4 us
    all_gather x1, blocking collectives, whole_of(): whole = lax.all_gather(whole, axes[number], axis=dim, tiled=True)  10.8 us
    another operation x1, loops' own time, shards(): lax.fori_loop(0, piece.shape[1], one_group, start_state)  10.2 us
  transfers between devices with their start and end apart: 3, of which 2 were waited for; matrix products, arithmetic and copies ran while one was open for 49% of the time, Pallas kernels for 0%

commit v1 on v0

--- a/solution.py
+++ b/solution.py
@@ -89,7 +89,23 @@
         jnp.zeros((prompts, rows, H), jnp.float32),
         jnp.zeros((prompts, rows, H, LAT), jnp.float32),
     )
-    piece = lax.all_gather(blended, "group", axis=1, tiled=True)
+    size, mine, span = (lax.axis_size("group"), lax.axis_index("group"), blended.shape[1])
+    upward = [(i, (i + 1) % size) for i in range(size)]
+    backward = [(i, (i - 1) % size) for i in range(size)]
+    piece = jnp.zeros((*blended.shape[:1], size * span, *blended.shape[1 + 1 :]), blended.dtype)
+    piece = lax.dynamic_update_slice_in_dim(piece, blended, mine * span, axis=1)
+    from_left = from_right = blended
+    middle = size // 2
+    for step in range(1, middle + 1):
+        from_left = lax.ppermute(from_left, "group", upward)
+        piece = lax.dynamic_update_slice_in_dim(
+            piece, from_left, (mine - step) % size * span, axis=1
+        )
+        if step < size - middle:
+            from_right = lax.ppermute(from_right, "group", backward)
+            piece = lax.dynamic_update_slice_in_dim(
+                piece, from_right, (mine + step) % size * span, axis=1
+            )
 
     def one_group(index, carry):
         keys = lax.dynamic_slice_in_dim(piece, index, 1, 1)[:, 0]

time: 242 us -> 201 us (0.83)
  the two profiles are of different devices: /device:TPU:57 before, /device:TPU:4 now
where the time goes in v1:
time: 201 us; the launch traced here: 199 us
  local copies, waits for them, and re-layouts  51.9 us (26%)
  matrix products  48.3 us (24%)
  waiting for transfers between devices  30.9 us (15%)
  other arithmetic  22.4 us (11%)
  blocking collectives  15.1 us (8%)
  between operations  14.3 us (7%)
  loops' own time  10.4 us (5%)
  starting transfers between devices  5.9 us (3%)
    dynamic_slice x16, local copies, waits for them, and re-layouts, one_group(): keys = lax.dynamic_slice_in_dim(piece, index, 1, 1)[:, 0]  26.2 us
    dot_general x8, matrix products, update(): jnp.einsum('pqhe,pke->pqhk', query_vec, keys, preferred_element_type=jnp....  20.3 us
    ppermute x4, waiting for transfers between devices, shards(): from_left = lax.ppermute(from_left, 'group', upward)  18 us
    dot_general x8, matrix products, update(): jnp.einsum('pqhk,pkl->pqhl', probs.astype(jnp.bfloat16), keys[..., :LAT],...  17.9 us
    all_gather x1, blocking collectives, whole_of(): whole = lax.all_gather(whole, axes[number], axis=dim, tiled=True)  15.1 us
    all_gather x1, waiting for transfers between devices, whole_of(): whole = lax.all_gather(whole, axes[number], axis=dim, tiled=True)  10.4 us
    another operation x1, loops' own time, shards(): lax.fori_loop(0, piece.shape[1], one_group, start_state)  9.77 us
    all_gather x1, local copies, waits for them, and re-layouts, whole_of(): whole = lax.all_gather(whole, axes[number], axis=dim, tiled=True)  6.48 us
  transfers between devices with their start and end apart: 9, of which 6 were waited for; matrix products, arithmetic and copies ran while one was open for 59% of the time, Pallas kernels for 0%

profile of v1, /device:TPU:4, one launch (start us, length us, event | category | flops | bytes accessed | tf_op | source)
XLA Modules:
  0.0 199.3 jit_solution(3622878935636186669)
XLA Ops:
  7.2 15.1 %all_gather.9 = bf16[64,4096]{1,0:T(8,128)(2,1)} all-gather(bf16[16,4096]{1,0:T(8,128)(2,1)} %param.18), channel_id=1, replica_groups=mesh['group'=8,'prompt_0'=8,'prompt_1'=4] {'prompt_1'}, dimensions={0}, use_global_device_ids=true | all-gather | bytes 655360 | tf_op jit(solution)/shard_map/all_gather | solution.py:19
  30.1 1.7 collective-permute-start.1
  31.8 7.6 %collective-permute-done = bf16[1,1,512,576]{2,3,1,0:T(8,128)(2,1)S(1)} collective-permute-done((bf16[1,1,512,576]{2,3,1,0:T(8,128)(2,1)S(1)}, bf16[1,1,512,576]{2,3,1,0:T(8,128)(2,1)S(1)}, u32[]{:S(2)}, u32[]{:S(2)}) %collective-permute-start) | collective-permute-done | bytes 589856 | tf_op jit(solution)/shard_map/ppermute | solution.py:100
  39.4 1.6 reshape.418
  41.8 1.8 collective-permute-start.3
  43.6 2.6 %broadcast_in_dim.59 = bf16[1,8,512,576]{2,3,1,0:T(8,128)(2,1)} broadcast(bf16[]{:T(256)} %constant.130.clone.1), dimensions={} | broadcast | bytes 4718594 | tf_op jit(solution)/shard_map/broadcast_in_dim | solution.py:95
  49.2 1.8 collective-permute-done.3
  51.0 2.3 %collective-permute-start.5 = (bf16[1,1,512,576]{2,3,1,0:T(8,128)(2,1)S(1)}, bf16[1,1,512,576]{2,3,1,0:T(8,128)(2,1)S(1)}, u32[]{:S(2)}, u32[]{:S(2)}) collective-permute-start(bf16[1,1,512,576]{2,3,1,0:T(8,128)(2,1)S(1)} %collective-permute-done.3), channel_id=1, source_target_pairs={{0,224},{32,0},{64,32},{96,64},{128,96},{160,128},{192,160},{224,1... | collective-permute-start | bytes 1769480 | tf_op jit(solution)/shard_map/ppermute | solution.py:105
  54.2 3.8 %collective-permute-done.4 = bf16[1,1,512,576]{2,3,1,0:T(8,128)(2,1)S(1)} collective-permute-done((bf16[1,1,512,576]{2,3,1,0:T(8,128)(2,1)S(1)}, bf16[1,1,512,576]{2,3,1,0:T(8,128)(2,1)S(1)}, u32[]{:S(2)}, u32[]{:S(2)}) %collective-permute-start.4) | collective-permute-done | bytes 589856 | tf_op jit(solution)/shard_map/ppermute | solution.py:100
  62.3 5.0 %collective-permute-done.6 = bf16[1,1,512,576]{2,3,1,0:T(8,128)(2,1)S(1)} collective-permute-done((bf16[1,1,512,576]{2,3,1,0:T(8,128)(2,1)S(1)}, bf16[1,1,512,576]{2,3,1,0:T(8,128)(2,1)S(1)}, u32[]{:S(2)}, u32[]{:S(2)}) %collective-permute-start.6) | collective-permute-done | bytes 589856 | tf_op jit(solution)/shard_map/ppermute | solution.py:100
  68.2 10.4 %all-gather.3.cloned.1.call-done = bf16[512,4096]{1,0:T(8,128)(2,1)} async-done(((bf16[64,4096]{1,0:T(8,128)(2,1)}), bf16[512,4096]{1,0:T(8,128)(2,1)}) %all-gather.3.cloned.1.call-update) | async-done | bytes 4194320 | tf_op jit(solution)/shard_map/all_gather | solution.py:19
  78.6 6.5 %copy.64 = bf16[512,4096]{0,1:T(8,128)(2,1)} copy(bf16[512,4096]{1,0:T(8,128)(2,1)} %all-gather.3.cloned.1.call-done) | data formatting | bytes 8388608 | tf_op jit(solution)/shard_map/all_gather | solution.py:19
  85.1 2.0 %fusion.20 = bf16[1,1,64,16,512]{4,2,3,1,0:T(8,128)(2,1)S(1)} fusion(bf16[512,16,256]{0,2,1:T(8,128)(2,1)} %bitcast.98, bf16[1,1,64,16,128]{4,3,2,1,0:T(8,128)(2,1)S(1)} %slice-done), kind=kOutput, calls=%fused_computation.31 | convolution fusion | flops 134742016 | bytes 3407872 | tf_op jit(solution)/shard_map/pcshd,lhd->pcshl/dot_general | solution.py:55
  88.8 95.1 %while.20 = (s32[]{:T(128)}, f32[1,64,16]{1,2,0:T(8,128)S(1)}, f32[1,64,16]{1,2,0:T(8,128)S(1)}, f32[1,64,16,512]{3,2,1,0:T(8,128)S(1)}, s32[1,8]{1,0:T(1,128)S(...) while((s32[]{:T(128)}, f32[1,64,16]{1,2,0:T(8,128)S(1)}, ...), condition=%wide.region_8.9_spmd.clone, body=%wide.region_3.8_spmd.clone.sunk | while | flops 1146129920 | bytes 17670692 | solution.py:117
  91.6 9.1 %conditional.3 = ((f32[1,64,16]{1,2,0:T(8,128)S(1)}, f32[1,64,16]{1,2,0:T(8,128)S(1)}, f32[1,64,16,512]{3,2,1,0:T(8,128)S(1)})) conditional(s32[]{:T(128)} %bitcast.96, (f32[1,64,16]{1,2,0:T(8,128)S(1)}, f32[1,64,16]{1,2,0:T(8,128)S(1)}, f32[1,64,16,512]{3,2,1,0:T(8,128)S(1)}) %tuple.66, (s32[1,512]{1,0:T(1,128)S(1)}, s32[1,1,64]{2,1,0:T(1,128)S(1)}, ...), branch_computations={%region_4.4_spmd, %region_5.0_spmd} | conditional | flops 1146129408 | bytes 17668416 | solution.py:115
  92.9 2.5 %fusion.2 = (f32[64,16]{0,1:T(8,128)S(1)}, f32[512,64,16]{0,1,2:T(8,128)S(1)}) fusion(pred[64,512]{1,0:T(8,128)(4,1)S(1)} %broadcast_compare_fusion, bf16[1,64,16,576]{3,1,2,0:T(8,128)(2,1)} %get-tuple-element.279, bf16[1,1,512,576]{2,3,1,0:T(8,128)(2,1)S(1)} %constant_dynamic-slice_fusion), kind=kOutput, calls=%fused_computation.5 | convolution fusion | flops 605551616 | bytes 3903488 | tf_op jit(solution)/shard_map/while/body/eval_jaxpr/cond/branch_1_fun/pqhe,pke->pqhk/dot_general | solution.py:71
  96.3 2.2 %copy.55 = bf16[1,1,512,576]{3,2,1,0:T(8,128)(2,1)} copy(bf16[1,1,512,576]{2,3,1,0:T(8,128)(2,1)} %copy-done) | data formatting | bytes 1179648 | tf_op jit(solution)/shard_map/while/body/eval_jaxpr/dynamic_slice | solution.py:111
  98.4 2.2 %bitcast_add_fusion = f32[1,64,16,512]{3,2,1,0:T(8,128)S(1)} fusion(f32[1,64,16,512]{3,2,1,0:T(8,128)S(1)} %get-tuple-element.281, bf16[64,16,512]{2,0,1:T(8,128)(2,1)S(1)} %get-tuple-element.353, f32[64,16]{1,0:T(8,128)S(1)} %copy.54, bf16[1,512,576]{2,1,0:T(8,128)(2,1)} %bitcast.97), kind=kOutput, calls=%fused_computation.2 | convolution fusion | flops 537919488 | bytes 5771264 | tf_op jit(solution)/shard_map/while/body/eval_jaxpr/cond/branch_1_fun/pqhk,pkl->pqhl/dot_general | solution.py:79
  103.5 9.0 %conditional.3 = ((f32[1,64,16]{1,2,0:T(8,128)S(1)}, f32[1,64,16]{1,2,0:T(8,128)S(1)}, f32[1,64,16,512]{3,2,1,0:T(8,128)S(1)})) conditional(s32[]{:T(128)} %bitcast.96, (f32[1,64,16]{1,2,0:T(8,128)S(1)}, f32[1,64,16]{1,2,0:T(8,128)S(1)}, f32[1,64,16,512]{3,2,1,0:T(8,128)S(1)}) %tuple.66, (s32[1,512]{1,0:T(1,128)S(1)}, s32[1,1,64]{2,1,0:T(1,128)S(1)}, ...), branch_computations={%region_4.4_spmd, %region_5.0_spmd} | conditional | flops 1146129408 | bytes 17668416 | solution.py:115
  104.8 2.5 %fusion.2 = (f32[64,16]{0,1:T(8,128)S(1)}, f32[512,64,16]{0,1,2:T(8,128)S(1)}) fusion(pred[64,512]{1,0:T(8,128)(4,1)S(1)} %broadcast_compare_fusion, bf16[1,64,16,576]{3,1,2,0:T(8,128)(2,1)} %get-tuple-element.279, bf16[1,1,512,576]{2,3,1,0:T(8,128)(2,1)S(1)} %constant_dynamic-slice_fusion), kind=kOutput, calls=%fused_computation.5 | convolution fusion | flops 605551616 | bytes 3903488 | tf_op jit(solution)/shard_map/while/body/eval_jaxpr/cond/branch_1_fun/pqhe,pke->pqhk/dot_general | solution.py:71
  108.1 2.2 %copy.55 = bf16[1,1,512,576]{3,2,1,0:T(8,128)(2,1)} copy(bf16[1,1,512,576]{2,3,1,0:T(8,128)(2,1)} %copy-done) | data formatting | bytes 1179648 | tf_op jit(solution)/shard_map/while/body/eval_jaxpr/dynamic_slice | solution.py:111
  110.3 2.2 %bitcast_add_fusion = f32[1,64,16,512]{3,2,1,0:T(8,128)S(1)} fusion(f32[1,64,16,512]{3,2,1,0:T(8,128)S(1)} %get-tuple-element.281, bf16[64,16,512]{2,0,1:T(8,128)(2,1)S(1)} %get-tuple-element.353, f32[64,16]{1,0:T(8,128)S(1)} %copy.54, bf16[1,512,576]{2,1,0:T(8,128)(2,1)} %bitcast.97), kind=kOutput, calls=%fused_computation.2 | convolution fusion | flops 537919488 | bytes 5771264 | tf_op jit(solution)/shard_map/while/body/eval_jaxpr/cond/branch_1_fun/pqhk,pkl->pqhl/dot_general | solution.py:79
  115.4 9.0 %conditional.3 = ((f32[1,64,16]{1,2,0:T(8,128)S(1)}, f32[1,64,16]{1,2,0:T(8,128)S(1)}, f32[1,64,16,512]{3,2,1,0:T(8,128)S(1)})) conditional(s32[]{:T(128)} %bitcast.96, (f32[1,64,16]{1,2,0:T(8,128)S(1)}, f32[1,64,16]{1,2,0:T(8,128)S(1)}, f32[1,64,16,512]{3,2,1,0:T(8,128)S(1)}) %tuple.66, (s32[1,512]{1,0:T(1,128)S(1)}, s32[1,1,64]{2,1,0:T(1,128)S(1)}, ...), branch_computations={%region_4.4_spmd, %region_5.0_spmd} | conditional | flops 1146129408 | bytes 17668416 | solution.py:115
  116.6 2.5 %fusion.2 = (f32[64,16]{0,1:T(8,128)S(1)}, f32[512,64,16]{0,1,2:T(8,128)S(1)}) fusion(pred[64,512]{1,0:T(8,128)(4,1)S(1)} %broadcast_compare_fusion, bf16[1,64,16,576]{3,1,2,0:T(8,128)(2,1)} %get-tuple-element.279, bf16[1,1,512,576]{2,3,1,0:T(8,128)(2,1)S(1)} %constant_dynamic-slice_fusion), kind=kOutput, calls=%fused_computation.5 | convolution fusion | flops 605551616 | bytes 3903488 | tf_op jit(solution)/shard_map/while/body/eval_jaxpr/cond/branch_1_fun/pqhe,pke->pqhk/dot_general | solution.py:71
  120.0 2.2 %copy.55 = bf16[1,1,512,576]{3,2,1,0:T(8,128)(2,1)} copy(bf16[1,1,512,576]{2,3,1,0:T(8,128)(2,1)} %copy-done) | data formatting | bytes 1179648 | tf_op jit(solution)/shard_map/while/body/eval_jaxpr/dynamic_slice | solution.py:111
  122.2 2.2 %bitcast_add_fusion = f32[1,64,16,512]{3,2,1,0:T(8,128)S(1)} fusion(f32[1,64,16,512]{3,2,1,0:T(8,128)S(1)} %get-tuple-element.281, bf16[64,16,512]{2,0,1:T(8,128)(2,1)S(1)} %get-tuple-element.353, f32[64,16]{1,0:T(8,128)S(1)} %copy.54, bf16[1,512,576]{2,1,0:T(8,128)(2,1)} %bitcast.97), kind=kOutput, calls=%fused_computation.2 | convolution fusion | flops 537919488 | bytes 5771264 | tf_op jit(solution)/shard_map/while/body/eval_jaxpr/cond/branch_1_fun/pqhk,pkl->pqhl/dot_general | solution.py:79
  127.3 9.0 %conditional.3 = ((f32[1,64,16]{1,2,0:T(8,128)S(1)}, f32[1,64,16]{1,2,0:T(8,128)S(1)}, f32[1,64,16,512]{3,2,1,0:T(8,128)S(1)})) conditional(s32[]{:T(128)} %bitcast.96, (f32[1,64,16]{1,2,0:T(8,128)S(1)}, f32[1,64,16]{1,2,0:T(8,128)S(1)}, f32[1,64,16,512]{3,2,1,0:T(8,128)S(1)}) %tuple.66, (s32[1,512]{1,0:T(1,128)S(1)}, s32[1,1,64]{2,1,0:T(1,128)S(1)}, ...), branch_computations={%region_4.4_spmd, %region_5.0_spmd} | conditional | flops 1146129408 | bytes 17668416 | solution.py:115
  128.5 2.5 %fusion.2 = (f32[64,16]{0,1:T(8,128)S(1)}, f32[512,64,16]{0,1,2:T(8,128)S(1)}) fusion(pred[64,512]{1,0:T(8,128)(4,1)S(1)} %broadcast_compare_fusion, bf16[1,64,16,576]{3,1,2,0:T(8,128)(2,1)} %get-tuple-element.279, bf16[1,1,512,576]{2,3,1,0:T(8,128)(2,1)S(1)} %constant_dynamic-slice_fusion), kind=kOutput, calls=%fused_computation.5 | convolution fusion | flops 605551616 | bytes 3903488 | tf_op jit(solution)/shard_map/while/body/eval_jaxpr/cond/branch_1_fun/pqhe,pke->pqhk/dot_general | solution.py:71
  131.8 2.2 %copy.55 = bf16[1,1,512,576]{3,2,1,0:T(8,128)(2,1)} copy(bf16[1,1,512,576]{2,3,1,0:T(8,128)(2,1)} %copy-done) | data formatting | bytes 1179648 | tf_op jit(solution)/shard_map/while/body/eval_jaxpr/dynamic_slice | solution.py:111
  134.0 2.2 %bitcast_add_fusion = f32[1,64,16,512]{3,2,1,0:T(8,128)S(1)} fusion(f32[1,64,16,512]{3,2,1,0:T(8,128)S(1)} %get-tuple-element.281, bf16[64,16,512]{2,0,1:T(8,128)(2,1)S(1)} %get-tuple-element.353, f32[64,16]{1,0:T(8,128)S(1)} %copy.54, bf16[1,512,576]{2,1,0:T(8,128)(2,1)} %bitcast.97), kind=kOutput, calls=%fused_computation.2 | convolution fusion | flops 537919488 | bytes 5771264 | tf_op jit(solution)/shard_map/while/body/eval_jaxpr/cond/branch_1_fun/pqhk,pkl->pqhl/dot_general | solution.py:79
  139.1 9.1 %conditional.3 = ((f32[1,64,16]{1,2,0:T(8,128)S(1)}, f32[1,64,16]{1,2,0:T(8,128)S(1)}, f32[1,64,16,512]{3,2,1,0:T(8,128)S(1)})) conditional(s32[]{:T(128)} %bitcast.96, (f32[1,64,16]{1,2,0:T(8,128)S(1)}, f32[1,64,16]{1,2,0:T(8,128)S(1)}, f32[1,64,16,512]{3,2,1,0:T(8,128)S(1)}) %tuple.66, (s32[1,512]{1,0:T(1,128)S(1)}, s32[1,1,64]{2,1,0:T(1,128)S(1)}, ...), branch_computations={%region_4.4_spmd, %region_5.0_spmd} | conditional | flops 1146129408 | bytes 17668416 | solution.py:115
  140.3 2.6 %fusion.2 = (f32[64,16]{0,1:T(8,128)S(1)}, f32[512,64,16]{0,1,2:T(8,128)S(1)}) fusion(pred[64,512]{1,0:T(8,128)(4,1)S(1)} %broadcast_compare_fusion, bf16[1,64,16,576]{3,1,2,0:T(8,128)(2,1)} %get-tuple-element.279, bf16[1,1,512,576]{2,3,1,0:T(8,128)(2,1)S(1)} %constant_dynamic-slice_fusion), kind=kOutput, calls=%fused_computation.5 | convolution fusion | flops 605551616 | bytes 3903488 | tf_op jit(solution)/shard_map/while/body/eval_jaxpr/cond/branch_1_fun/pqhe,pke->pqhk/dot_general | solution.py:71
  143.7 2.2 %copy.55 = bf16[1,1,512,576]{3,2,1,0:T(8,128)(2,1)} copy(bf16[1,1,512,576]{2,3,1,0:T(8,128)(2,1)} %copy-done) | data formatting | bytes 1179648 | tf_op jit(solution)/shard_map/while/body/eval_jaxpr/dynamic_slice | solution.py:111
  145.9 2.3 %bitcast_add_fusion = f32[1,64,16,512]{3,2,1,0:T(8,128)S(1)} fusion(f32[1,64,16,512]{3,2,1,0:T(8,128)S(1)} %get-tuple-element.281, bf16[64,16,512]{2,0,1:T(8,128)(2,1)S(1)} %get-tuple-element.353, f32[64,16]{1,0:T(8,128)S(1)} %copy.54, bf16[1,512,576]{2,1,0:T(8,128)(2,1)} %bitcast.97), kind=kOutput, calls=%fused_computation.2 | convolution fusion | flops 537919488 | bytes 5771264 | tf_op jit(solution)/shard_map/while/body/eval_jaxpr/cond/branch_1_fun/pqhk,pkl->pqhl/dot_general | solution.py:79
  151.0 9.1 %conditional.3 = ((f32[1,64,16]{1,2,0:T(8,128)S(1)}, f32[1,64,16]{1,2,0:T(8,128)S(1)}, f32[1,64,16,512]{3,2,1,0:T(8,128)S(1)})) conditional(s32[]{:T(128)} %bitcast.96, (f32[1,64,16]{1,2,0:T(8,128)S(1)}, f32[1,64,16]{1,2,0:T(8,128)S(1)}, f32[1,64,16,512]{3,2,1,0:T(8,128)S(1)}) %tuple.66, (s32[1,512]{1,0:T(1,128)S(1)}, s32[1,1,64]{2,1,0:T(1,128)S(1)}, ...), branch_computations={%region_4.4_spmd, %region_5.0_spmd} | conditional | flops 1146129408 | bytes 17668416 | solution.py:115
  152.3 2.6 %fusion.2 = (f32[64,16]{0,1:T(8,128)S(1)}, f32[512,64,16]{0,1,2:T(8,128)S(1)}) fusion(pred[64,512]{1,0:T(8,128)(4,1)S(1)} %broadcast_compare_fusion, bf16[1,64,16,576]{3,1,2,0:T(8,128)(2,1)} %get-tuple-element.279, bf16[1,1,512,576]{2,3,1,0:T(8,128)(2,1)S(1)} %constant_dynamic-slice_fusion), kind=kOutput, calls=%fused_computation.5 | convolution fusion | flops 605551616 | bytes 3903488 | tf_op jit(solution)/shard_map/while/body/eval_jaxpr/cond/branch_1_fun/pqhe,pke->pqhk/dot_general | solution.py:71
  155.7 2.2 %copy.55 = bf16[1,1,512,576]{3,2,1,0:T(8,128)(2,1)} copy(bf16[1,1,512,576]{2,3,1,0:T(8,128)(2,1)} %copy-done) | data formatting | bytes 1179648 | tf_op jit(solution)/shard_map/while/body/eval_jaxpr/dynamic_slice | solution.py:111
  157.8 2.3 %bitcast_add_fusion = f32[1,64,16,512]{3,2,1,0:T(8,128)S(1)} fusion(f32[1,64,16,512]{3,2,1,0:T(8,128)S(1)} %get-tuple-element.281, bf16[64,16,512]{2,0,1:T(8,128)(2,1)S(1)} %get-tuple-element.353, f32[64,16]{1,0:T(8,128)S(1)} %copy.54, bf16[1,512,576]{2,1,0:T(8,128)(2,1)} %bitcast.97), kind=kOutput, calls=%fused_computation.2 | convolution fusion | flops 537919488 | bytes 5771264 | tf_op jit(solution)/shard_map/while/body/eval_jaxpr/cond/branch_1_fun/pqhk,pkl->pqhl/dot_general | solution.py:79
  163.0 9.0 %conditional.3 = ((f32[1,64,16]{1,2,0:T(8,128)S(1)}, f32[1,64,16]{1,2,0:T(8,128)S(1)}, f32[1,64,16,512]{3,2,1,0:T(8,128)S(1)})) conditional(s32[]{:T(128)} %bitcast.96, (f32[1,64,16]{1,2,0:T(8,128)S(1)}, f32[1,64,16]{1,2,0:T(8,128)S(1)}, f32[1,64,16,512]{3,2,1,0:T(8,128)S(1)}) %tuple.66, (s32[1,512]{1,0:T(1,128)S(1)}, s32[1,1,64]{2,1,0:T(1,128)S(1)}, ...), branch_computations={%region_4.4_spmd, %region_5.0_spmd} | conditional | flops 1146129408 | bytes 17668416 | solution.py:115
  164.2 2.5 %fusion.2 = (f32[64,16]{0,1:T(8,128)S(1)}, f32[512,64,16]{0,1,2:T(8,128)S(1)}) fusion(pred[64,512]{1,0:T(8,128)(4,1)S(1)} %broadcast_compare_fusion, bf16[1,64,16,576]{3,1,2,0:T(8,128)(2,1)} %get-tuple-element.279, bf16[1,1,512,576]{2,3,1,0:T(8,128)(2,1)S(1)} %constant_dynamic-slice_fusion), kind=kOutput, calls=%fused_computation.5 | convolution fusion | flops 605551616 | bytes 3903488 | tf_op jit(solution)/shard_map/while/body/eval_jaxpr/cond/branch_1_fun/pqhe,pke->pqhk/dot_general | solution.py:71
  167.6 2.2 %copy.55 = bf16[1,1,512,576]{3,2,1,0:T(8,128)(2,1)} copy(bf16[1,1,512,576]{2,3,1,0:T(8,128)(2,1)} %copy-done) | data formatting | bytes 1179648 | tf_op jit(solution)/shard_map/while/body/eval_jaxpr/dynamic_slice | solution.py:111
  169.7 2.2 %bitcast_add_fusion = f32[1,64,16,512]{3,2,1,0:T(8,128)S(1)} fusion(f32[1,64,16,512]{3,2,1,0:T(8,128)S(1)} %get-tuple-element.281, bf16[64,16,512]{2,0,1:T(8,128)(2,1)S(1)} %get-tuple-element.353, f32[64,16]{1,0:T(8,128)S(1)} %copy.54, bf16[1,512,576]{2,1,0:T(8,128)(2,1)} %bitcast.97), kind=kOutput, calls=%fused_computation.2 | convolution fusion | flops 537919488 | bytes 5771264 | tf_op jit(solution)/shard_map/while/body/eval_jaxpr/cond/branch_1_fun/pqhk,pkl->pqhl/dot_general | solution.py:79
  174.8 9.0 %conditional.3 = ((f32[1,64,16]{1,2,0:T(8,128)S(1)}, f32[1,64,16]{1,2,0:T(8,128)S(1)}, f32[1,64,16,512]{3,2,1,0:T(8,128)S(1)})) conditional(s32[]{:T(128)} %bitcast.96, (f32[1,64,16]{1,2,0:T(8,128)S(1)}, f32[1,64,16]{1,2,0:T(8,128)S(1)}, f32[1,64,16,512]{3,2,1,0:T(8,128)S(1)}) %tuple.66, (s32[1,512]{1,0:T(1,128)S(1)}, s32[1,1,64]{2,1,0:T(1,128)S(1)}, ...), branch_computations={%region_4.4_spmd, %region_5.0_spmd} | conditional | flops 1146129408 | bytes 17668416 | solution.py:115
  176.1 2.5 %fusion.2 = (f32[64,16]{0,1:T(8,128)S(1)}, f32[512,64,16]{0,1,2:T(8,128)S(1)}) fusion(pred[64,512]{1,0:T(8,128)(4,1)S(1)} %broadcast_compare_fusion, bf16[1,64,16,576]{3,1,2,0:T(8,128)(2,1)} %get-tuple-element.279, bf16[1,1,512,576]{2,3,1,0:T(8,128)(2,1)S(1)} %constant_dynamic-slice_fusion), kind=kOutput, calls=%fused_computation.5 | convolution fusion | flops 605551616 | bytes 3903488 | tf_op jit(solution)/shard_map/while/body/eval_jaxpr/cond/branch_1_fun/pqhe,pke->pqhk/dot_general | solution.py:71
  179.4 2.2 %copy.55 = bf16[1,1,512,576]{3,2,1,0:T(8,128)(2,1)} copy(bf16[1,1,512,576]{2,3,1,0:T(8,128)(2,1)} %copy-done) | data formatting | bytes 1179648 | tf_op jit(solution)/shard_map/while/body/eval_jaxpr/dynamic_slice | solution.py:111
  181.6 2.2 %bitcast_add_fusion = f32[1,64,16,512]{3,2,1,0:T(8,128)S(1)} fusion(f32[1,64,16,512]{3,2,1,0:T(8,128)S(1)} %get-tuple-element.281, bf16[64,16,512]{2,0,1:T(8,128)(2,1)S(1)} %get-tuple-element.353, f32[64,16]{1,0:T(8,128)S(1)} %copy.54, bf16[1,512,576]{2,1,0:T(8,128)(2,1)} %bitcast.97), kind=kOutput, calls=%fused_computation.2 | convolution fusion | flops 537919488 | bytes 5771264 | tf_op jit(solution)/shard_map/while/body/eval_jaxpr/cond/branch_1_fun/pqhk,pkl->pqhl/dot_general | solution.py:79
  184.1 2.4 %fusion.26 = bf16[1,64,16,128]{3,1,2,0:T(8,128)(2,1)S(1)} fusion(bf16[512,16,256]{0,2,1:T(8,128)(2,1)} %bitcast.99, bf16[64,16,512]{2,1,0:T(8,128)(2,1)S(1)} %fusion.30), kind=kOutput, calls=%fused_computation.34 | convolution fusion | flops 134348800 | bytes 3407872 | tf_op jit(solution)/shard_map/pqhl,lhv->pqhv/dot_general | solution.py:119
  186.8 5.7 %fusion.12 = bf16[1,1,64,2048]{3,2,1,0:T(8,128)(2,1)} fusion(bf16[2048,2048]{1,0:T(8,128)(2,1)} %all-gather.5.cloned.1.call-done, bf16[8,8,16,128]{3,2,1,0:T(8,128)(2,1)S(1)} %bitcast.103), kind=kOutput, calls=%fused_computation.24 | convolution fusion | flops 537001984 | bytes 8912896 | tf_op jit(solution)/shard_map/dot_general | solution.py:124
  (158 shorter events, 48.7 us)
Async XLA Ops:
  7.2 21.1 %copy-start.3 = (bf16[1,1,64,576]{3,2,1,0:T(8,128)(2,1)S(1)}, bf16[1,1,64,576]{3,2,1,0:T(8,128)(2,1)}, u32[]{:S(2)}) copy-start(bf16[1,1,64,576]{3,2,1,0:T(8,128)(2,1)} %param.13) | copy-start | bytes 221188
  7.2 21.0 %copy-start.4 = (bf16[512]{0:T(512)(128)(2,1)S(1)}, bf16[512]{0:T(512)(128)(2,1)}, u32[]{:S(2)}) copy-start(bf16[512]{0:T(512)(128)(2,1)} %param.17) | copy-start | bytes 3076
  7.2 71.5 %all-gather.3.cloned.1.call-start = ((), (), s32[]{:S(2)}) async-start(), calls=%async_computation | async-start | bytes 4718592 | tf_op jit(solution)/shard_map/all_gather | solution.py:19
  22.3 164.4 %all-gather.5.cloned.1.call-start = ((), (), s32[]{:S(2)}) async-start(), calls=%async_computation.1 | async-start | bytes 8650752 | tf_op jit(solution)/shard_map/all_gather | solution.py:123
  30.1 16.2 %copy-start.1 = (bf16[1,1,512,576]{2,3,1,0:T(8,128)(2,1)}, bf16[1,1,512,576]{2,3,1,0:T(8,128)(2,1)S(1)}, u32[]{:S(2)}) copy-start(bf16[1,1,512,576]{2,3,1,0:T(8,128)(2,1)S(1)} %copy.61) | copy-start | bytes 1769476
  30.1 9.3 %collective-permute-start = (bf16[1,1,512,576]{2,3,1,0:T(8,128)(2,1)S(1)}, bf16[1,1,512,576]{2,3,1,0:T(8,128)(2,1)S(1)}, u32[]{:S(2)}, u32[]{:S(2)}) collective-permute-start(bf16[1,1,512,576]{2,3,1,0:T(8,128)(2,1)S(1)} %copy.61), channel_id=1, source_target_pairs={{0,32},{32,64},{64,96},{96,128},{128,160},{160,192},{192,224},{224... | collective-permute-start | bytes 1769480 | tf_op jit(solution)/shard_map/ppermute | solution.py:100
  30.1 11.7 %collective-permute-start.1 = (bf16[1,1,512,576]{2,3,1,0:T(8,128)(2,1)S(1)}, bf16[1,1,512,576]{2,3,1,0:T(8,128)(2,1)S(1)}, u32[]{:S(2)}, u32[]{:S(2)}) collective-permute-start(bf16[1,1,512,576]{2,3,1,0:T(8,128)(2,1)S(1)} %copy.61), channel_id=1, source_target_pairs={{0,224},{32,0},{64,32},{96,64},{128,96},{160,128},{192,160},{224,1... | collective-permute-start | bytes 1769480 | tf_op jit(solution)/shard_map/ppermute | solution.py:105
  39.4 9.3 %collective-permute-start.2 = (bf16[1,1,512,576]{2,3,1,0:T(8,128)(2,1)S(1)}, bf16[1,1,512,576]{2,3,1,0:T(8,128)(2,1)S(1)}, u32[]{:S(2)}, u32[]{:S(2)}) collective-permute-start(bf16[1,1,512,576]{2,3,1,0:T(8,128)(2,1)S(1)} %collective-permute-done), channel_id=1, source_target_pairs={{0,32},{32,64},{64,96},{96,128},{128,160},{160,192},{192,224},{224... | collective-permute-start | bytes 1769480 | tf_op jit(solution)/shard_map/ppermute | solution.py:100
  41.0 5.2 %copy-start.2 = (bf16[1,1,64,16,192]{4,3,2,1,0:T(8,128)(2,1)}, bf16[1,1,64,16,192]{4,3,2,1,0:T(8,128)(2,1)S(1)}, u32[]{:S(2)}) copy-start(bf16[1,1,64,16,192]{4,3,2,1,0:T(8,128)(2,1)S(1)} %reshape.418) | copy-start | bytes 1179652
  41.8 9.2 %collective-permute-start.3 = (bf16[1,1,512,576]{2,3,1,0:T(8,128)(2,1)S(1)}, bf16[1,1,512,576]{2,3,1,0:T(8,128)(2,1)S(1)}, u32[]{:S(2)}, u32[]{:S(2)}) collective-permute-start(bf16[1,1,512,576]{2,3,1,0:T(8,128)(2,1)S(1)} %collective-permute-done.1), channel_id=1, source_target_pairs={{0,224},{32,0},{64,32},{96,64},{128,96},{160,128},{192,160},{224,1... | collective-permute-start | bytes 1769480 | tf_op jit(solution)/shard_map/ppermute | solution.py:105
  48.7 9.3 %collective-permute-start.4 = (bf16[1,1,512,576]{2,3,1,0:T(8,128)(2,1)S(1)}, bf16[1,1,512,576]{2,3,1,0:T(8,128)(2,1)S(1)}, u32[]{:S(2)}, u32[]{:S(2)}) collective-permute-start(bf16[1,1,512,576]{2,3,1,0:T(8,128)(2,1)S(1)} %collective-permute-done.2), channel_id=1, source_target_pairs={{0,32},{32,64},{64,96},{96,128},{128,160},{160,192},{192,224},{224... | collective-permute-start | bytes 1769480 | tf_op jit(solution)/shard_map/ppermute | solution.py:100
  51.0 10.4 %collective-permute-start.5 = (bf16[1,1,512,576]{2,3,1,0:T(8,128)(2,1)S(1)}, bf16[1,1,512,576]{2,3,1,0:T(8,128)(2,1)S(1)}, u32[]{:S(2)}, u32[]{:S(2)}) collective-permute-start(bf16[1,1,512,576]{2,3,1,0:T(8,128)(2,1)S(1)} %collective-permute-done.3), channel_id=1, source_target_pairs={{0,224},{32,0},{64,32},{96,64},{128,96},{160,128},{192,160},{224,1... | collective-permute-start | bytes 1769480 | tf_op jit(solution)/shard_map/ppermute | solution.py:105
  58.0 9.3 %collective-permute-start.6 = (bf16[1,1,512,576]{2,3,1,0:T(8,128)(2,1)S(1)}, bf16[1,1,512,576]{2,3,1,0:T(8,128)(2,1)S(1)}, u32[]{:S(2)}, u32[]{:S(2)}) collective-permute-start(bf16[1,1,512,576]{2,3,1,0:T(8,128)(2,1)S(1)} %collective-permute-done.4), channel_id=1, source_target_pairs={{0,32},{32,64},{64,96},{96,128},{128,160},{160,192},{192,224},{224... | collective-permute-start | bytes 1769480 | tf_op jit(solution)/shard_map/ppermute | solution.py:100
  68.2 16.9 %slice-start = ((bf16[1,1,64,16,192]{4,3,2,1,0:T(8,128)(2,1)}), bf16[1,1,64,16,128]{4,3,2,1,0:T(8,128)(2,1)S(1)}, s32[]{:S(2)}) async-start(bf16[1,1,64,16,192]{4,3,2,1,0:T(8,128)(2,1)} %copy-done.2), calls=%async_computation.2 | async-start | bytes 524288 | tf_op jit(solution)/shard_map/slice | solution.py:56
  87.2 1.6 copy-start.5
  92.8 2.7 %copy-start = (bf16[1,1,512,576]{2,3,1,0:T(8,128)(2,1)}, bf16[1,1,512,576]{2,3,1,0:T(8,128)(2,1)S(1)}, u32[]{:S(2)}) copy-start(bf16[1,1,512,576]{2,3,1,0:T(8,128)(2,1)S(1)} %constant_dynamic-slice_fusion) | copy-start | bytes 1769476 | tf_op jit(solution)/shard_map/while/body/eval_jaxpr/cond
  104.7 2.6 %copy-start = (bf16[1,1,512,576]{2,3,1,0:T(8,128)(2,1)}, bf16[1,1,512,576]{2,3,1,0:T(8,128)(2,1)S(1)}, u32[]{:S(2)}) copy-start(bf16[1,1,512,576]{2,3,1,0:T(8,128)(2,1)S(1)} %constant_dynamic-slice_fusion) | copy-start | bytes 1769476 | tf_op jit(solution)/shard_map/while/body/eval_jaxpr/cond
  116.5 2.6 %copy-start = (bf16[1,1,512,576]{2,3,1,0:T(8,128)(2,1)}, bf16[1,1,512,576]{2,3,1,0:T(8,128)(2,1)S(1)}, u32[]{:S(2)}) copy-start(bf16[1,1,512,576]{2,3,1,0:T(8,128)(2,1)S(1)} %constant_dynamic-slice_fusion) | copy-start | bytes 1769476 | tf_op jit(solution)/shard_map/while/body/eval_jaxpr/cond
  128.4 2.6 %copy-start = (bf16[1,1,512,576]{2,3,1,0:T(8,128)(2,1)}, bf16[1,1,512,576]{2,3,1,0:T(8,128)(2,1)S(1)}, u32[]{:S(2)}) copy-start(bf16[1,1,512,576]{2,3,1,0:T(8,128)(2,1)S(1)} %constant_dynamic-slice_fusion) | copy-start | bytes 1769476 | tf_op jit(solution)/shard_map/while/body/eval_jaxpr/cond
  140.2 2.7 %copy-start = (bf16[1,1,512,576]{2,3,1,0:T(8,128)(2,1)}, bf16[1,1,512,576]{2,3,1,0:T(8,128)(2,1)S(1)}, u32[]{:S(2)}) copy-start(bf16[1,1,512,576]{2,3,1,0:T(8,128)(2,1)S(1)} %constant_dynamic-slice_fusion) | copy-start | bytes 1769476 | tf_op jit(solution)/shard_map/while/body/eval_jaxpr/cond
  152.2 2.7 %copy-start = (bf16[1,1,512,576]{2,3,1,0:T(8,128)(2,1)}, bf16[1,1,512,576]{2,3,1,0:T(8,128)(2,1)S(1)}, u32[]{:S(2)}) copy-start(bf16[1,1,512,576]{2,3,1,0:T(8,128)(2,1)S(1)} %constant_dynamic-slice_fusion) | copy-start | bytes 1769476 | tf_op jit(solution)/shard_map/while/body/eval_jaxpr/cond
  164.1 2.6 %copy-start = (bf16[1,1,512,576]{2,3,1,0:T(8,128)(2,1)}, bf16[1,1,512,576]{2,3,1,0:T(8,128)(2,1)S(1)}, u32[]{:S(2)}) copy-start(bf16[1,1,512,576]{2,3,1,0:T(8,128)(2,1)S(1)} %constant_dynamic-slice_fusion) | copy-start | bytes 1769476 | tf_op jit(solution)/shard_map/while/body/eval_jaxpr/cond
  176.0 2.6 %copy-start = (bf16[1,1,512,576]{2,3,1,0:T(8,128)(2,1)}, bf16[1,1,512,576]{2,3,1,0:T(8,128)(2,1)S(1)}, u32[]{:S(2)}) copy-start(bf16[1,1,512,576]{2,3,1,0:T(8,128)(2,1)S(1)} %constant_dynamic-slice_fusion) | copy-start | bytes 1769476 | tf_op jit(solution)/shard_map/while/body/eval_jaxpr/cond
Sparse Core Ops, SparseCore 0:
  22.5 56.1 all-gather.2
  81.2 96.5 all-gather.4
